TPU v7x, 32 devices: a whole 2x2x4 slice. The times are simulated.
32 devices in a mesh: tm: 2 (over x), grid: 16 (over z, y, core).
Axes of the slice: x: 2, y: 2, z: 4, core: 2. Of those that a mesh axis runs over, the one named last changes fastest.
Arguments:
- occupied_green: bfloat16 [2, 1024, 1024], P('tm', 'grid'), may hold values from -0.005859375 to 0.005859375
- empty_green: bfloat16 [2, 1024, 1024], P('tm', 'grid'), may hold values from -0.005859375 to 0.005859375
- basis: bfloat16 [12288, 1024], P('grid'), may hold values from -8 to 8
- time_weights: float32 [2, 2], replicated, may hold values from 0.25 to 1
Outputs:
- polarizability: float32 [2, 1024, 1024], P('tm', 'grid')
All inputs are finite; a program needn't handle non-finite values.
Results may differ from a plain program's by a relative error of at most 0.0012.
Values may be sent and summed in bfloat16 or wider, within the bound.
A program may use at most 128 MiB of HBM per device.

v0:
```python
import jax
import jax.numpy as jnp
from jax import lax
from jax.sharding import PartitionSpec as P

NR = 12288
NB = 1024


def weigh_times(time_weights, block_list, scale_factor):
    time_count = len(block_list)
    group_index = lax.axis_index("tm")
    weights_local = lax.dynamic_slice_in_dim(time_weights, group_index * time_count, time_count, 1)
    accum = weights_local[:, 0, None, None] * block_list[0][None]
    return scale_factor * accum


def step_size(piece_rows):
    return max((divisor for divisor in range(1, 2049) if piece_rows % divisor == 0))


def shards(occupied_green, empty_green, basis, time_weights):
    stacked = jnp.stack([occupied_green, empty_green])
    time_count = occupied_green.shape[0]
    coef_block = occupied_green.shape[1]
    row_total = basis.shape[0]
    scale_factor = 1.0 / NR

    def make_accumulate(combined_rows):

        def accumulate(running, basis_piece, first_row):
            piece_rows = basis_piece.shape[0]
            step_rows = step_size(piece_rows)

            def one_step(step_index, inner):
                basis_subpart = lax.dynamic_slice_in_dim(
                    basis_piece, step_index * step_rows, step_rows, 0
                )
                real_pair = jnp.einsum(
                    "qoa,ba->qob", combined_rows, basis_subpart, preferred_element_type=jnp.float32
                )
                product = (real_pair[0] * real_pair[1]).astype(jnp.bfloat16)
                return inner + jnp.dot(product, basis_subpart, preferred_element_type=jnp.float32)

            return lax.fori_loop(0, piece_rows // step_rows, one_step, running)

        return accumulate

    initial = jnp.zeros((time_count * row_total, NB), jnp.float32)
    projected = jnp.einsum(
        "sl,ftkl->ftsk",
        basis,
        lax.all_gather(stacked, "grid", axis=2, tiled=True),
        preferred_element_type=jnp.float32,
    ).astype(jnp.bfloat16)
    combined_rows = projected.reshape(2, time_count * row_total, NB)
    accumulate = make_accumulate(combined_rows)
    summed = accumulate(initial, lax.all_gather(basis, "grid", axis=0, tiled=True), jnp.int32(0))
    back_half = summed.astype(jnp.bfloat16).reshape(time_count, row_total, NB)
    coef_rows = lax.psum_scatter(
        jnp.einsum("tsk,sl->ktl", back_half, basis, preferred_element_type=jnp.float32).reshape(
            lax.axis_size("grid") * coef_block, time_count * NB
        ),
        "grid",
        scatter_dimension=0,
        tiled=True,
    ).reshape(coef_block, time_count, NB)
    block_list = [coef_rows[:, 0]]
    result = lax.psum_scatter(
        weigh_times(time_weights, block_list, scale_factor), "tm", scatter_dimension=0, tiled=True
    )
    return result


def solution(mesh):
    in_specs = (P("tm", "grid", None), P("tm", "grid", None), P("grid", None), P())
    out_specs = P("tm", "grid", None)
    return jax.shard_map(shards, mesh=mesh, in_specs=in_specs, out_specs=out_specs, check_vma=False)
```

profile of v0, /device:TPU:0, one launch (start us, length us, event | category | flops | bytes accessed | tf_op | source)
XLA Modules:
  0.0 431.6 jit_solution(16188916720244867342)
XLA Ops:
  6.5 1.7 pad_maximum_fusion
  8.3 0.7 all-gather.3.cloned.1.call-update
  9.1 53.6 %all-gather.5.cloned.1.call-done = bf16[2,1,1024,1024]{3,2,0,1:T(8,128)(2,1)} async-done(((bf16[2,1,64,1024]{3,2,0,1:T(8,128)(2,1)}), bf16[2,1,1024,1024]{3,2,0,1:T(8,128)(2,1)}) %all-gather.5.cloned.1.call-update) | async-done | bytes 4194320 | tf_op jit(solution)/shard_map/all_gather | solution.py:53
  62.7 7.9 %convert_bitcast_fusion = bf16[2,768,1024]{1,2,0:T(8,128)(2,1)} fusion(bf16[2,1,1024,1024]{3,2,0,1:T(8,128)(2,1)} %all-gather.5.cloned.1.call-done, bf16[768,1024]{1,0:T(8,128)(2,1)} %param.8), kind=kOutput, calls=%fused_computation.13 | convolution fusion | flops 3222798336 | bytes 8912896 | tf_op jit(solution)/shard_map/sl,ftkl->ftsk/dot_general | solution.py:50
  70.5 3.2 copy.5
  73.8 117.6 %all-gather.3.cloned.1.call-done = bf16[12288,1024]{1,0:T(8,128)(2,1)} async-done(((bf16[768,1024]{1,0:T(8,128)(2,1)}), bf16[12288,1024]{1,0:T(8,128)(2,1)}) %all-gather.3.cloned.1.call-update) | async-done | bytes 25165840 | tf_op jit(solution)/shard_map/all_gather | solution.py:58
  191.3 138.8 %while.14 = (s32[]{:T(128)}, f32[768,1024]{1,0:T(8,128)}, bf16[12288,1024]{1,0:T(8,128)(2,1)}, bf16[2,768,1024]{2,1,0:T(8,128)(2,1)S(1)}, s32[]{:T(128)}, /*index=5*/s32[]{:T(128)}, s32[]{:T(128)}, s32[]{:T(128)}) while((s32[]{:T(128)}, f32[768,1024]{1,0:T(8,128)}, bf16[12288,1024]{1,0:T(8,128)(2,1)}, ...), condition=%wide.region_1.0_spmd.clone, body=%wide.region_0.0_spmd.clone.sunk | while | flops 9668395008 | bytes 42991772 | solution.py:45
  191.4 11.5 %convolution_bitcast_fusion.2 = f32[2,768,2048]{1,2,0:T(8,128)} fusion(bf16[2,768,1024]{2,1,0:T(8,128)(2,1)S(1)} %get-tuple-element.156, bf16[12288,1024]{1,0:T(8,128)(2,1)} %get-tuple-element.155, s32[]{:T(128)S(6)} %select_n.13), kind=kOutput, calls=%fused_computation.2.clone.1 | convolution fusion | flops 6442450944 | bytes 19922948 | tf_op jit(solution)/shard_map/while/body/eval_jaxpr/qoa,ba->qob/dot_general | solution.py:39
  202.9 10.9 %select_add_fusion.2 = f32[768,1024]{1,0:T(8,128)} fusion(f32[768,1024]{1,0:T(8,128)} %get-tuple-element.146, bf16[12288,1024]{1,0:T(8,128)(2,1)} %get-tuple-element.155, s32[]{:T(128)S(6)} %select_n.13, f32[2,768,2048]{1,2,0:T(8,128)} %convolution_bitcast_fusion.2, pred[]{:T(512)S(6)} %compare.3), kind=kOutput, calls=%fused_computation.8.clone.1 | convolution fusion | flops 3225944064 | bytes 23068676 | tf_op jit(solution)/shard_map/while/body/eval_jaxpr/dot_general | solution.py:43
  213.7 11.5 %convolution_bitcast_fusion.2 = f32[2,768,2048]{1,2,0:T(8,128)} fusion(bf16[2,768,1024]{2,1,0:T(8,128)(2,1)S(1)} %get-tuple-element.156, bf16[12288,1024]{1,0:T(8,128)(2,1)} %get-tuple-element.155, s32[]{:T(128)S(6)} %select_n.13), kind=kOutput, calls=%fused_computation.2.clone.1 | convolution fusion | flops 6442450944 | bytes 19922948 | tf_op jit(solution)/shard_map/while/body/eval_jaxpr/qoa,ba->qob/dot_general | solution.py:39
  225.2 11.8 %select_add_fusion.2 = f32[768,1024]{1,0:T(8,128)} fusion(f32[768,1024]{1,0:T(8,128)} %get-tuple-element.146, bf16[12288,1024]{1,0:T(8,128)(2,1)} %get-tuple-element.155, s32[]{:T(128)S(6)} %select_n.13, f32[2,768,2048]{1,2,0:T(8,128)} %convolution_bitcast_fusion.2, pred[]{:T(512)S(6)} %compare.3), kind=kOutput, calls=%fused_computation.8.clone.1 | convolution fusion | flops 3225944064 | bytes 23068676 | tf_op jit(solution)/shard_map/while/body/eval_jaxpr/dot_general | solution.py:43
  237.0 11.5 %convolution_bitcast_fusion.2 = f32[2,768,2048]{1,2,0:T(8,128)} fusion(bf16[2,768,1024]{2,1,0:T(8,128)(2,1)S(1)} %get-tuple-element.156, bf16[12288,1024]{1,0:T(8,128)(2,1)} %get-tuple-element.155, s32[]{:T(128)S(6)} %select_n.13), kind=kOutput, calls=%fused_computation.2.clone.1 | convolution fusion | flops 6442450944 | bytes 19922948 | tf_op jit(solution)/shard_map/while/body/eval_jaxpr/qoa,ba->qob/dot_general | solution.py:39
  248.5 11.8 %select_add_fusion.2 = f32[768,1024]{1,0:T(8,128)} fusion(f32[768,1024]{1,0:T(8,128)} %get-tuple-element.146, bf16[12288,1024]{1,0:T(8,128)(2,1)} %get-tuple-element.155, s32[]{:T(128)S(6)} %select_n.13, f32[2,768,2048]{1,2,0:T(8,128)} %convolution_bitcast_fusion.2, pred[]{:T(512)S(6)} %compare.3), kind=kOutput, calls=%fused_computation.8.clone.1 | convolution fusion | flops 3225944064 | bytes 23068676 | tf_op jit(solution)/shard_map/while/body/eval_jaxpr/dot_general | solution.py:43
  260.3 11.5 %convolution_bitcast_fusion.2 = f32[2,768,2048]{1,2,0:T(8,128)} fusion(bf16[2,768,1024]{2,1,0:T(8,128)(2,1)S(1)} %get-tuple-element.156, bf16[12288,1024]{1,0:T(8,128)(2,1)} %get-tuple-element.155, s32[]{:T(128)S(6)} %select_n.13), kind=kOutput, calls=%fused_computation.2.clone.1 | convolution fusion | flops 6442450944 | bytes 19922948 | tf_op jit(solution)/shard_map/while/body/eval_jaxpr/qoa,ba->qob/dot_general | solution.py:39
  271.8 11.8 %select_add_fusion.2 = f32[768,1024]{1,0:T(8,128)} fusion(f32[768,1024]{1,0:T(8,128)} %get-tuple-element.146, bf16[12288,1024]{1,0:T(8,128)(2,1)} %get-tuple-element.155, s32[]{:T(128)S(6)} %select_n.13, f32[2,768,2048]{1,2,0:T(8,128)} %convolution_bitcast_fusion.2, pred[]{:T(512)S(6)} %compare.3), kind=kOutput, calls=%fused_computation.8.clone.1 | convolution fusion | flops 3225944064 | bytes 23068676 | tf_op jit(solution)/shard_map/while/body/eval_jaxpr/dot_general | solution.py:43
  283.6 11.5 %convolution_bitcast_fusion.2 = f32[2,768,2048]{1,2,0:T(8,128)} fusion(bf16[2,768,1024]{2,1,0:T(8,128)(2,1)S(1)} %get-tuple-element.156, bf16[12288,1024]{1,0:T(8,128)(2,1)} %get-tuple-element.155, s32[]{:T(128)S(6)} %select_n.13), kind=kOutput, calls=%fused_computation.2.clone.1 | convolution fusion | flops 6442450944 | bytes 19922948 | tf_op jit(solution)/shard_map/while/body/eval_jaxpr/qoa,ba->qob/dot_general | solution.py:39
  295.1 11.8 %select_add_fusion.2 = f32[768,1024]{1,0:T(8,128)} fusion(f32[768,1024]{1,0:T(8,128)} %get-tuple-element.146, bf16[12288,1024]{1,0:T(8,128)(2,1)} %get-tuple-element.155, s32[]{:T(128)S(6)} %select_n.13, f32[2,768,2048]{1,2,0:T(8,128)} %convolution_bitcast_fusion.2, pred[]{:T(512)S(6)} %compare.3), kind=kOutput, calls=%fused_computation.8.clone.1 | convolution fusion | flops 3225944064 | bytes 23068676 | tf_op jit(solution)/shard_map/while/body/eval_jaxpr/dot_general | solution.py:43
  306.9 11.5 %convolution_bitcast_fusion.2 = f32[2,768,2048]{1,2,0:T(8,128)} fusion(bf16[2,768,1024]{2,1,0:T(8,128)(2,1)S(1)} %get-tuple-element.156, bf16[12288,1024]{1,0:T(8,128)(2,1)} %get-tuple-element.155, s32[]{:T(128)S(6)} %select_n.13), kind=kOutput, calls=%fused_computation.2.clone.1 | convolution fusion | flops 6442450944 | bytes 19922948 | tf_op jit(solution)/shard_map/while/body/eval_jaxpr/qoa,ba->qob/dot_general | solution.py:39
  318.4 11.8 %select_add_fusion.2 = f32[768,1024]{1,0:T(8,128)} fusion(f32[768,1024]{1,0:T(8,128)} %get-tuple-element.146, bf16[12288,1024]{1,0:T(8,128)(2,1)} %get-tuple-element.155, s32[]{:T(128)S(6)} %select_n.13, f32[2,768,2048]{1,2,0:T(8,128)} %convolution_bitcast_fusion.2, pred[]{:T(512)S(6)} %compare.3), kind=kOutput, calls=%fused_computation.8.clone.1 | convolution fusion | flops 3225944064 | bytes 23068676 | tf_op jit(solution)/shard_map/while/body/eval_jaxpr/dot_general | solution.py:43
  330.2 6.1 %fusion.18 = f32[1024,1024]{1,0:T(8,128)} fusion(bf16[768,1024]{1,0:T(8,128)(2,1)} %param.8, f32[768,1024]{1,0:T(8,128)} %get-tuple-element.84), kind=kOutput, calls=%fused_computation.15 | convolution fusion | flops 1611399168 | bytes 8912896 | tf_op jit(solution)/shard_map/tsk,sl->ktl/dot_general | solution.py:61
  336.4 0.2 dynamic-slice_reduce_fusion
  336.6 72.7 %reduce-scatter.3.cloned.1.call-done = f32[64,1024]{1,0:T(8,128)} async-done(((f32[1024,1024]{1,0:T(8,128)}), f32[64,1024]{1,0:T(8,128)}) %reduce-scatter.3.cloned.1.call-update) | async-done | bytes 262160 | tf_op jit(solution)/shard_map/reduce_scatter | solution.py:60
  409.2 1.9 multiply_multiply_fusion
  411.1 13.9 %reduce-scatter.5.cloned.1.call-done = f32[1,64,1024]{2,1,0:T(8,128)} async-done(((f32[2,64,1024]{2,1,0:T(8,128)}), f32[1,64,1024]{2,1,0:T(8,128)}) %reduce-scatter.5.cloned.1.call-update) | async-done | bytes 262160 | tf_op jit(solution)/shard_map/reduce_scatter | solution.py:69
  (10 shorter events, 0.2 us)
Async XLA Ops:
  6.5 329.8 %copy-start = (f32[2,2]{1,0:T(2,128)S(1)}, f32[2,2]{1,0:T(2,128)}, u32[]{:S(2)}) copy-start(f32[2,2]{1,0:T(2,128)} %param.9) | copy-start | bytes 52
  6.5 56.1 %all-gather.5.cloned.1.call-start = ((), (), s32[]{:S(2)}) async-start(), calls=%async_computation.3 | async-start | bytes 4456448 | tf_op jit(solution)/shard_map/all_gather | solution.py:53
  8.3 183.1 %all-gather.3.cloned.1.call-start = ((), (), s32[]{:S(2)}) async-start(), calls=%async_computation.2 | async-start | bytes 26738688 | tf_op jit(solution)/shard_map/all_gather | solution.py:58
  9.0 400.2 %reduce-scatter.3.cloned.1.call-start = ((), (), s32[]{:S(2)}) async-start(), calls=%async_computation.4 | async-start | bytes 4456448 | tf_op jit(solution)/shard_map/reduce_scatter | solution.py:60
  336.3 88.8 %reduce-scatter.5.cloned.1.call-start = ((), (), s32[]{:S(2)}) async-start(), calls=%async_computation.5 | async-start | bytes 786432 | tf_op jit(solution)/shard_map/reduce_scatter | solution.py:69
Sparse Core Ops, SparseCore 0:
  9.5 53.1 all-gather.4
  64.3 127.0 all-gather.2
  336.4 72.7 reduce-scatter.2
  411.3 13.6 reduce-scatter.4
where the time goes:
time: 432 us
  waiting for transfers between devices  259 us (60%)
  matrix products  153 us (35%)
  between operations  13.2 us (3%)
    all_gather x1, waiting for transfers between devices, shards(): lax.all_gather(basis, 'grid', axis=0, tiled=True)  118 us
    reduce_scatter x1, waiting for transfers between devices, shards(): lax.psum_scatter(jnp.einsum('tsk,sl->ktl', back_half, basis, preferred_el...  72.7 us
    dot_general x6, matrix products, one_step(): jnp.dot(product, basis_subpart, preferred_element_type=jnp.float32)  69.8 us
    dot_general x6, matrix products, one_step(): jnp.einsum('qoa,ba->qob', combined_rows, basis_subpart, preferred_element...  69 us
    all_gather x1, waiting for transfers between devices, shards(): lax.all_gather(stacked, 'grid', axis=2, tiled=True)  53.6 us
    reduce_scatter x1, waiting for transfers between devices, shards(): lax.psum_scatter(weigh_times(time_weights, block_list, scale_factor), 'tm...  13.9 us
  transfers between devices with their start and end apart: 4, of which 4 were waited for; matrix products, arithmetic and copies ran while one was open for 3% of the time, Pallas kernels for 0%

commit v1 on v0

--- a/solution.py
+++ b/solution.py
@@ -2,9 +2,18 @@
 import jax.numpy as jnp
 from jax import lax
 from jax.sharding import PartitionSpec as P
+from jax.lax import all_to_all, psum
 
 NR = 12288
 NB = 1024
+
+
+def draw_classes_up(u_in):
+    b_now = tuple((u_in for _ in range(psum(1, "grid"))))
+    newest = jnp.stack(b_now)
+    inter = all_to_all(newest, "grid", 0, 0)
+    top = jnp.concatenate(inter, 2)
+    return top
 
 
 def weigh_times(time_weights, block_list, scale_factor):
@@ -48,10 +57,7 @@
 
     initial = jnp.zeros((time_count * row_total, NB), jnp.float32)
     projected = jnp.einsum(
-        "sl,ftkl->ftsk",
-        basis,
-        lax.all_gather(stacked, "grid", axis=2, tiled=True),
-        preferred_element_type=jnp.float32,
+        "sl,ftkl->ftsk", basis, draw_classes_up(stacked), preferred_element_type=jnp.float32
     ).astype(jnp.bfloat16)
     combined_rows = projected.reshape(2, time_count * row_total, NB)
     accumulate = make_accumulate(combined_rows)

time: 432 us -> 470 us (1.088)
  waiting for transfers between devices: 259 us -> 288 us
  starting transfers between devices: 0.12 us -> 7.55 us
  local copies, waits for them, and re-layouts: 3.4 us -> 8.61 us
    all_to_all x0 -> x1, waiting for transfers between devices: none -> 141 us  [draw_classes_up(): inter = all_to_all(newest, 'grid', 0, 0)]
    all_gather x1, waiting for transfers between devices: 118 us -> 49.8 us  [shards(): lax.all_gather(basis, 'grid', axis=0, tiled=True)]
    all_gather x1 -> x0, waiting for transfers between devices: 53.6 us -> none  [shards(): lax.all_gather(stacked, 'grid', axis=2, tiled=True)]
    reduce_scatter x1, waiting for transfers between devices: 72.7 us -> 82 us  [shards(): lax.psum_scatter(jnp.einsum('tsk,sl->ktl', back_half, basis, preferred_el...]
    all_to_all x0 -> x1, starting transfers between devices: none -> 7.46 us  [draw_classes_up(): inter = all_to_all(newest, 'grid', 0, 0)]
where the time goes in v1:
time: 470 us
  waiting for transfers between devices  288 us (61%)
  matrix products  150 us (32%)
  between operations  13.2 us (3%)
  local copies, waits for them, and re-layouts  8.61 us (2%)
  starting transfers between devices  7.55 us (2%)
    all_to_all x1, waiting for transfers between devices, draw_classes_up(): inter = all_to_all(newest, 'grid', 0, 0)  141 us
    reduce_scatter x1, waiting for transfers between devices, shards(): lax.psum_scatter(jnp.einsum('tsk,sl->ktl', back_half, basis, preferred_el...  82 us
    dot_general x6, matrix products, one_step(): jnp.dot(product, basis_subpart, preferred_element_type=jnp.float32)  69.8 us
    dot_general x6, matrix products, one_step(): jnp.einsum('qoa,ba->qob', combined_rows, basis_subpart, preferred_element...  69 us
    all_gather x1, waiting for transfers between devices, shards(): lax.all_gather(basis, 'grid', axis=0, tiled=True)  49.8 us
    reduce_scatter x1, waiting for transfers between devices, shards(): lax.psum_scatter(weigh_times(time_weights, block_list, scale_factor), 'tm...  14.1 us
  transfers between devices with their start and end apart: 4, of which 4 were waited for; matrix products, arithmetic and copies ran while one was open for 3% of the time, Pallas kernels for 0%

profile of v1, /device:TPU:0, one launch (start us, length us, event | category | flops | bytes accessed | tf_op | source)
XLA Modules:
  0.0 469.6 jit_solution(2461877737687091937)
XLA Ops:
  8.3 2.5 stack.14
  10.7 7.5 %all-to-all-start = ((bf16[16,2,1,64,1024]{4,3,1,2,0:T(8,128)(2,1)}), bf16[16,2,1,64,1024]{4,3,1,2,0:T(8,128)(2,1)}, u32[]{:S(2)}, u32[]{:S(2)}) async-start(bf16[16,2,1,64,1024]{4,3,1,2,0:T(8,128)(2,1)} %stack.14), calls=%async_computation | async-start | bytes 8388608 | tf_op jit(solution)/shard_map/all_to_all | solution.py:14
  18.3 141.0 %all-to-all-done = bf16[16,2,1,64,1024]{4,3,1,2,0:T(8,128)(2,1)} async-done(((bf16[16,2,1,64,1024]{4,3,1,2,0:T(8,128)(2,1)}), bf16[16,2,1,64,1024]{4,3,1,2,0:T(8,128)(2,1)}, u32[]{:S(2)}, u32[]{:S(2)}) %all-to-all-start) | async-done | bytes 4194336 | tf_op jit(solution)/shard_map/all_to_all | solution.py:14
  159.2 2.7 copy.6
  162.0 4.8 %convert_bitcast_fusion = bf16[2,768,1024]{1,2,0:T(8,128)(2,1)} fusion(bf16[2,1024,1024]{2,1,0:T(8,128)(2,1)S(1)} %bitcast.36, bf16[768,1024]{1,0:T(8,128)(2,1)S(1)} %copy-done.1), kind=kOutput, calls=%fused_computation.11 | convolution fusion | flops 3222798336 | bytes 8912896 | tf_op jit(solution)/shard_map/sl,ftkl->ftsk/dot_general | solution.py:59
  166.8 3.2 copy.7
  170.0 49.8 %all-gather.2.cloned.1.call-done = bf16[12288,1024]{1,0:T(8,128)(2,1)} async-done(((bf16[768,1024]{1,0:T(8,128)(2,1)}), bf16[12288,1024]{1,0:T(8,128)(2,1)}) %all-gather.2.cloned.1.call-update) | async-done | bytes 25165840 | tf_op jit(solution)/shard_map/all_gather | solution.py:64
  219.9 138.8 %while.14 = (s32[]{:T(128)}, f32[768,1024]{1,0:T(8,128)}, bf16[12288,1024]{1,0:T(8,128)(2,1)}, bf16[2,768,1024]{2,1,0:T(8,128)(2,1)S(1)}, s32[]{:T(128)}, /*index=5*/s32[]{:T(128)}, s32[]{:T(128)}, s32[]{:T(128)}) while((s32[]{:T(128)}, f32[768,1024]{1,0:T(8,128)}, bf16[12288,1024]{1,0:T(8,128)(2,1)}, ...), condition=%wide.region_1.0_spmd.clone, body=%wide.region_0.0_spmd.clone.sunk | while | flops 9668395008 | bytes 42991772 | solution.py:54
  219.9 11.5 %convolution_bitcast_fusion.2 = f32[2,768,2048]{1,2,0:T(8,128)} fusion(bf16[2,768,1024]{2,1,0:T(8,128)(2,1)S(1)} %get-tuple-element.160, bf16[12288,1024]{1,0:T(8,128)(2,1)} %get-tuple-element.159, s32[]{:T(128)S(6)} %select_n.13), kind=kOutput, calls=%fused_computation.2.clone.1 | convolution fusion | flops 6442450944 | bytes 19922948 | tf_op jit(solution)/shard_map/while/body/eval_jaxpr/qoa,ba->qob/dot_general | solution.py:48
  231.4 10.9 %select_add_fusion.2 = f32[768,1024]{1,0:T(8,128)} fusion(f32[768,1024]{1,0:T(8,128)} %get-tuple-element.150, bf16[12288,1024]{1,0:T(8,128)(2,1)} %get-tuple-element.159, s32[]{:T(128)S(6)} %select_n.13, f32[2,768,2048]{1,2,0:T(8,128)} %convolution_bitcast_fusion.2, pred[]{:T(512)S(6)} %compare.3), kind=kOutput, calls=%fused_computation.8.clone.1 | convolution fusion | flops 3225944064 | bytes 23068676 | tf_op jit(solution)/shard_map/while/body/eval_jaxpr/dot_general | solution.py:52
  242.3 11.5 %convolution_bitcast_fusion.2 = f32[2,768,2048]{1,2,0:T(8,128)} fusion(bf16[2,768,1024]{2,1,0:T(8,128)(2,1)S(1)} %get-tuple-element.160, bf16[12288,1024]{1,0:T(8,128)(2,1)} %get-tuple-element.159, s32[]{:T(128)S(6)} %select_n.13), kind=kOutput, calls=%fused_computation.2.clone.1 | convolution fusion | flops 6442450944 | bytes 19922948 | tf_op jit(solution)/shard_map/while/body/eval_jaxpr/qoa,ba->qob/dot_general | solution.py:48
  253.8 11.8 %select_add_fusion.2 = f32[768,1024]{1,0:T(8,128)} fusion(f32[768,1024]{1,0:T(8,128)} %get-tuple-element.150, bf16[12288,1024]{1,0:T(8,128)(2,1)} %get-tuple-element.159, s32[]{:T(128)S(6)} %select_n.13, f32[2,768,2048]{1,2,0:T(8,128)} %convolution_bitcast_fusion.2, pred[]{:T(512)S(6)} %compare.3), kind=kOutput, calls=%fused_computation.8.clone.1 | convolution fusion | flops 3225944064 | bytes 23068676 | tf_op jit(solution)/shard_map/while/body/eval_jaxpr/dot_general | solution.py:52
  265.5 11.5 %convolution_bitcast_fusion.2 = f32[2,768,2048]{1,2,0:T(8,128)} fusion(bf16[2,768,1024]{2,1,0:T(8,128)(2,1)S(1)} %get-tuple-element.160, bf16[12288,1024]{1,0:T(8,128)(2,1)} %get-tuple-element.159, s32[]{:T(128)S(6)} %select_n.13), kind=kOutput, calls=%fused_computation.2.clone.1 | convolution fusion | flops 6442450944 | bytes 19922948 | tf_op jit(solution)/shard_map/while/body/eval_jaxpr/qoa,ba->qob/dot_general | solution.py:48
  277.0 11.8 %select_add_fusion.2 = f32[768,1024]{1,0:T(8,128)} fusion(f32[768,1024]{1,0:T(8,128)} %get-tuple-element.150, bf16[12288,1024]{1,0:T(8,128)(2,1)} %get-tuple-element.159, s32[]{:T(128)S(6)} %select_n.13, f32[2,768,2048]{1,2,0:T(8,128)} %convolution_bitcast_fusion.2, pred[]{:T(512)S(6)} %compare.3), kind=kOutput, calls=%fused_computation.8.clone.1 | convolution fusion | flops 3225944064 | bytes 23068676 | tf_op jit(solution)/shard_map/while/body/eval_jaxpr/dot_general | solution.py:52
  288.8 11.5 %convolution_bitcast_fusion.2 = f32[2,768,2048]{1,2,0:T(8,128)} fusion(bf16[2,768,1024]{2,1,0:T(8,128)(2,1)S(1)} %get-tuple-element.160, bf16[12288,1024]{1,0:T(8,128)(2,1)} %get-tuple-element.159, s32[]{:T(128)S(6)} %select_n.13), kind=kOutput, calls=%fused_computation.2.clone.1 | convolution fusion | flops 6442450944 | bytes 19922948 | tf_op jit(solution)/shard_map/while/body/eval_jaxpr/qoa,ba->qob/dot_general | solution.py:48
  300.3 11.8 %select_add_fusion.2 = f32[768,1024]{1,0:T(8,128)} fusion(f32[768,1024]{1,0:T(8,128)} %get-tuple-element.150, bf16[12288,1024]{1,0:T(8,128)(2,1)} %get-tuple-element.159, s32[]{:T(128)S(6)} %select_n.13, f32[2,768,2048]{1,2,0:T(8,128)} %convolution_bitcast_fusion.2, pred[]{:T(512)S(6)} %compare.3), kind=kOutput, calls=%fused_computation.8.clone.1 | convolution fusion | flops 3225944064 | bytes 23068676 | tf_op jit(solution)/shard_map/while/body/eval_jaxpr/dot_general | solution.py:52
  312.1 11.5 %convolution_bitcast_fusion.2 = f32[2,768,2048]{1,2,0:T(8,128)} fusion(bf16[2,768,1024]{2,1,0:T(8,128)(2,1)S(1)} %get-tuple-element.160, bf16[12288,1024]{1,0:T(8,128)(2,1)} %get-tuple-element.159, s32[]{:T(128)S(6)} %select_n.13), kind=kOutput, calls=%fused_computation.2.clone.1 | convolution fusion | flops 6442450944 | bytes 19922948 | tf_op jit(solution)/shard_map/while/body/eval_jaxpr/qoa,ba->qob/dot_general | solution.py:48
  323.6 11.8 %select_add_fusion.2 = f32[768,1024]{1,0:T(8,128)} fusion(f32[768,1024]{1,0:T(8,128)} %get-tuple-element.150, bf16[12288,1024]{1,0:T(8,128)(2,1)} %get-tuple-element.159, s32[]{:T(128)S(6)} %select_n.13, f32[2,768,2048]{1,2,0:T(8,128)} %convolution_bitcast_fusion.2, pred[]{:T(512)S(6)} %compare.3), kind=kOutput, calls=%fused_computation.8.clone.1 | convolution fusion | flops 3225944064 | bytes 23068676 | tf_op jit(solution)/shard_map/while/body/eval_jaxpr/dot_general | solution.py:52
  335.4 11.5 %convolution_bitcast_fusion.2 = f32[2,768,2048]{1,2,0:T(8,128)} fusion(bf16[2,768,1024]{2,1,0:T(8,128)(2,1)S(1)} %get-tuple-element.160, bf16[12288,1024]{1,0:T(8,128)(2,1)} %get-tuple-element.159, s32[]{:T(128)S(6)} %select_n.13), kind=kOutput, calls=%fused_computation.2.clone.1 | convolution fusion | flops 6442450944 | bytes 19922948 | tf_op jit(solution)/shard_map/while/body/eval_jaxpr/qoa,ba->qob/dot_general | solution.py:48
  346.9 11.8 %select_add_fusion.2 = f32[768,1024]{1,0:T(8,128)} fusion(f32[768,1024]{1,0:T(8,128)} %get-tuple-element.150, bf16[12288,1024]{1,0:T(8,128)(2,1)} %get-tuple-element.159, s32[]{:T(128)S(6)} %select_n.13, f32[2,768,2048]{1,2,0:T(8,128)} %convolution_bitcast_fusion.2, pred[]{:T(512)S(6)} %compare.3), kind=kOutput, calls=%fused_computation.8.clone.1 | convolution fusion | flops 3225944064 | bytes 23068676 | tf_op jit(solution)/shard_map/while/body/eval_jaxpr/dot_general | solution.py:52
  358.7 6.1 %fusion.14 = f32[1024,1024]{1,0:T(8,128)} fusion(bf16[768,1024]{1,0:T(8,128)(2,1)} %param.8, f32[768,1024]{1,0:T(8,128)} %get-tuple-element.84), kind=kOutput, calls=%fused_computation.13 | convolution fusion | flops 1611399168 | bytes 8912896 | tf_op jit(solution)/shard_map/tsk,sl->ktl/dot_general | solution.py:67
  365.1 82.0 %reduce-scatter.3.cloned.1.call-done = f32[64,1024]{1,0:T(8,128)} async-done(((f32[1024,1024]{1,0:T(8,128)}), f32[64,1024]{1,0:T(8,128)}) %reduce-scatter.3.cloned.1.call-update) | async-done | bytes 262160 | tf_op jit(solution)/shard_map/reduce_scatter | solution.py:66
  447.1 1.9 multiply_multiply_fusion
  448.9 14.1 %reduce-scatter.5.cloned.1.call-done = f32[1,64,1024]{2,1,0:T(8,128)} async-done(((f32[2,64,1024]{2,1,0:T(8,128)}), f32[1,64,1024]{2,1,0:T(8,128)}) %reduce-scatter.5.cloned.1.call-update) | async-done | bytes 262160 | tf_op jit(solution)/shard_map/reduce_scatter | solution.py:75
  (13 shorter events, 2.0 us)
Async XLA Ops:
  6.5 358.4 %copy-start = (f32[2,2]{1,0:T(2,128)S(1)}, f32[2,2]{1,0:T(2,128)}, u32[]{:S(2)}) copy-start(f32[2,2]{1,0:T(2,128)} %param.9) | copy-start | bytes 52
  6.5 213.3 %all-gather.2.cloned.1.call-start = ((), (), s32[]{:S(2)}) async-start(), calls=%async_computation.3 | async-start | bytes 26738688 | tf_op jit(solution)/shard_map/all_gather | solution.py:64
  10.7 148.5 %all-to-all-start = ((bf16[16,2,1,64,1024]{4,3,1,2,0:T(8,128)(2,1)}), bf16[16,2,1,64,1024]{4,3,1,2,0:T(8,128)(2,1)}, u32[]{:S(2)}, u32[]{:S(2)}) async-start(bf16[16,2,1,64,1024]{4,3,1,2,0:T(8,128)(2,1)} %stack.14), calls=%async_computation | async-start | bytes 8388608 | tf_op jit(solution)/shard_map/all_to_all | solution.py:14
  18.2 428.9 %reduce-scatter.3.cloned.1.call-start = ((), (), s32[]{:S(2)}) async-start(), calls=%async_computation.4 | async-start | bytes 4456448 | tf_op jit(solution)/shard_map/reduce_scatter | solution.py:66
  159.2 2.8 copy-start.1
  364.8 98.2 %reduce-scatter.5.cloned.1.call-start = ((), (), s32[]{:S(2)}) async-start(), calls=%async_computation.5 | async-start | bytes 786432 | tf_op jit(solution)/shard_map/reduce_scatter | solution.py:75
Sparse Core Ops, SparseCore 0:
  8.9 210.8 all-gather.1
  364.9 82.0 reduce-scatter.2
  449.3 13.6 reduce-scatter.4
